TPU v7x, 512 devices: a whole 4x4x16 slice. The times are simulated.
512 devices in a mesh: section: 4 (over x), trial: 128 (over z, y, core).
Axes of the slice: x: 4, y: 4, z: 16, core: 2. Of those that a mesh axis runs over, the one named last changes fastest.
Arguments:
- spike_rates: bfloat16 [512, 256, 256], P(None, 'trial'), may hold values from -6 to 6
- first_preactivation: bfloat16 [1024, 256, 256], P('section', 'trial'), may hold values from -6 to 6
- second_preactivation: bfloat16 [1024, 256, 256], P('section', 'trial'), may hold values from -6 to 6
- output_gradient: bfloat16 [1024, 256, 256], P('section', 'trial'), may hold values from -0.29882812 to 0.29882812
- first_kernel: bfloat16 [3, 1024, 1024], P(None, None, 'section'), may hold values from -0.109375 to 0.109375
- second_kernel: bfloat16 [3, 1024, 1024], P(None, None, 'section'), may hold values from -0.109375 to 0.109375
- session_of: int32 [256], P('trial'), may hold values from 0 to 127, never falling along the last dimension, each value on 1 to 6 neighbouring positions
Outputs:
- readin_grad: bfloat16 [128, 512, 1024], P(None, 'trial', 'section')
Inputs may be any that keep to these rules, and one draw needn't show every extreme that they name: `session_of`: the trials of a session are consecutive; every session has 1 to 6 trials, and one has exactly 6.
All inputs are finite; a program needn't handle non-finite values.
Results may differ from a plain program's by a relative error of at most 0.017.
Values may be sent and summed in bfloat16 or wider, within the bound.
No kernel may reach another device: no remote copies, remote signals or barrier semaphores. Data moves between devices by JAX's collectives and lax.ppermute only.
A program may use at most 64 MiB of HBM per device.

v0:
```python
import math
import jax
import jax.numpy as jnp
from jax import lax
from jax.sharding import PartitionSpec as P

FIRST_DILATION = 32
SECOND_DILATION = 64
MOST = 6


def gelu_slope(preact):
    values = preact.astype(jnp.float32)
    normal_cdf = 0.5 * (1.0 + lax.erf(values * (1.0 / math.sqrt(2.0))))
    density = jnp.exp(-0.5 * values * values) * (1.0 / math.sqrt(2.0 * math.pi))
    return normal_cdf + values * density


def shift_ahead(values, offset):
    padding = [(0, 0)] * (values.ndim - 1) + [(0, offset)]
    return jnp.pad(values[..., offset:], padding)


def tap_sum(weights, flow_grad, spacing):
    running = None
    for kernel_tap in range(3):
        term_tap = lax.dot_general(
            weights[kernel_tap],
            flow_grad,
            (((1,), (0,)), ((), ())),
            preferred_element_type=jnp.float32,
        )
        if kernel_tap > 0:
            term_tap = shift_ahead(term_tap, kernel_tap * spacing)
        running = term_tap if running is None else running + term_tap
    return running


def layer_backprop(upstream, preact, turned, spacing):
    flow_grad = (upstream.astype(jnp.float32) * gelu_slope(preact)).astype(jnp.bfloat16)
    back_sum = tap_sum(turned, lax.all_gather(flow_grad, "section", axis=0, tiled=True), spacing)
    return (upstream.astype(jnp.float32) + back_sum).astype(jnp.bfloat16)


def body(
    spike_rates,
    first_preactivation,
    second_preactivation,
    output_gradient,
    first_kernel,
    second_kernel,
    session_of,
):
    first_flipped_kernel, second_flipped_kernel = (
        lax.all_to_all(first_kernel, "section", split_axis=1, concat_axis=2, tiled=True),
        lax.all_to_all(second_kernel, "section", split_axis=1, concat_axis=2, tiled=True),
    )
    upstream_gradient = layer_backprop(
        output_gradient, second_preactivation, second_flipped_kernel, SECOND_DILATION
    )
    input_gradient = layer_backprop(
        upstream_gradient, first_preactivation, first_flipped_kernel, FIRST_DILATION
    )
    trial_shards = lax.axis_size("trial")
    neurons, trials, steps_count = spike_rates.shape
    neuron_blocks = spike_rates.reshape(trial_shards, neurons // trial_shards, trials, steps_count)
    partials = jnp.einsum(
        "jbil,cil->jibc", neuron_blocks, input_gradient, preferred_element_type=jnp.float32
    )
    arrived = lax.all_to_all(
        partials.astype(jnp.bfloat16), "trial", split_axis=0, concat_axis=0, tiled=True
    ).astype(partials.dtype)
    every_id = lax.all_gather(session_of, "trial", axis=0, tiled=True)
    total_trials = every_id.shape[0]
    flat_parts = arrived.reshape(total_trials, -1)
    session_list = jnp.arange(trial_shards, dtype=jnp.int32)
    first_trial = jnp.sum((every_id[None, :] < session_list[:, None]).astype(jnp.int32), axis=1)

    def add_offset(offset, running):
        position = first_trial + offset
        clipped = jnp.minimum(position, total_trials - 1)
        rows_here = jnp.take(flat_parts, clipped, axis=0)
        valid = (position < total_trials) & (jnp.take(every_id, clipped, axis=0) == session_list)
        return running + jnp.where(valid[:, None], rows_here, 0.0)

    start_sums = jnp.zeros((trial_shards, flat_parts.shape[1]), jnp.float32)
    summed = lax.fori_loop(0, MOST, add_offset, start_sums)
    return summed.reshape(trial_shards, neurons // trial_shards, input_gradient.shape[0]).astype(
        jnp.bfloat16
    )


def solution(mesh):
    in_specs = (
        P(None, "trial", None),
        P("section", "trial", None),
        P("section", "trial", None),
        P("section", "trial", None),
        P(None, None, "section"),
        P(None, None, "section"),
        P("trial"),
    )
    out_specs = P(None, "trial", "section")
    return jax.shard_map(body, mesh=mesh, in_specs=in_specs, out_specs=out_specs, check_vma=False)
```

profile of v0, /device:TPU:8, one launch (start us, length us, event | category | flops | bytes accessed | tf_op | source)
XLA Modules:
  0.0 186.1 jit_solution(364001516441620479)
XLA Ops:
  6.5 0.0 copy-start
  6.5 0.0 all-gather.3.cloned.1.call-start
  6.5 1.2 copy.50
  7.8 1.1 copy.51
  8.9 1.0 fusion.14
  9.9 0.0 all-gather.3.cloned.1.call-update
  9.9 0.0 copy-done.3
  9.9 2.7 %copy.52 = bf16[3,1024,256]{2,0,1:T(4,128)(2,1)} copy(bf16[3,1024,256]{2,1,0:T(8,128)(2,1)S(1)} %copy-done.3) | data formatting | bytes 3145728 | tf_op args[5]
  12.6 4.4 %all-to-all-start = ((bf16[3,1024,256]{2,0,1:T(4,128)(2,1)}), bf16[3,1024,256]{2,0,1:T(4,128)(2,1)S(1)}, u32[]{:S(2)}, u32[]{:S(2)}) async-start(bf16[3,1024,256]{2,0,1:T(4,128)(2,1)} %copy.52), calls=%async_computation | async-start | bytes 4194304 | tf_op jit(solution)/shard_map/all_to_all | solution.py:56
  17.0 0.0 all-gather.5.cloned.1.call-start
  17.0 0.2 copy.54
  17.2 29.0 %all-to-all-done = bf16[3,1024,256]{2,0,1:T(4,128)(2,1)S(1)} async-done(((bf16[3,1024,256]{2,0,1:T(4,128)(2,1)}), bf16[3,1024,256]{2,0,1:T(4,128)(2,1)S(1)}, u32[]{:S(2)}, u32[]{:S(2)}) %all-to-all-start) | async-done | bytes 1572896 | tf_op jit(solution)/shard_map/all_to_all | solution.py:56
  46.2 1.5 copy.79
  47.7 0.5 fusion.34
  48.2 0.4 reshape.105
  48.6 0.4 reshape.106
  49.0 0.4 reshape.104
  49.4 6.2 %all-gather.3.cloned.1.call-done = bf16[1024,2,256]{0,2,1:T(8,128)(2,1)} async-done(((bf16[256,2,256]{0,2,1:T(8,128)(2,1)}), bf16[1024,2,256]{0,2,1:T(8,128)(2,1)}) %all-gather.3.cloned.1.call-update) | async-done | bytes 1048592 | tf_op jit(solution)/shard_map/all_gather | solution.py:41
  55.6 1.8 convolution_bitcast_fusion.4
  57.4 0.5 convolution_bitcast_fusion.3
  57.9 0.0 copy-start.4
  57.9 1.5 fusion.31
  59.4 0.0 all-gather.5.cloned.1.call-update
  59.4 0.0 copy-done.4
  59.4 1.4 copy.55
  60.8 31.6 %all_to_all.35 = bf16[3,1024,256]{2,0,1:T(4,128)(2,1)S(1)} all-to-all(bf16[3,1024,256]{2,0,1:T(4,128)(2,1)S(1)} %copy.55), channel_id=1, replica_groups=mesh['section'=4,'trial'=128] {'section'}, dimensions={1} | all-to-all | bytes 3145728 | tf_op jit(solution)/shard_map/all_to_all | solution.py:55
  92.3 0.2 copy.56
  92.6 0.1 fusion.33
  92.7 0.2 copy.59
  92.9 0.2 copy.61
  93.1 0.2 copy.57
  93.3 7.2 %all-gather.5.cloned.1.call-done = bf16[1024,2,256]{0,2,1:T(8,128)(2,1)} async-done(((bf16[256,2,256]{0,2,1:T(8,128)(2,1)}), bf16[1024,2,256]{0,2,1:T(8,128)(2,1)}) %all-gather.5.cloned.1.call-update) | async-done | bytes 1048592 | tf_op jit(solution)/shard_map/all_gather | solution.py:41
  100.5 1.8 convolution_bitcast_fusion.1
  102.3 0.4 convolution_bitcast_fusion
  102.8 2.0 %fusion.3 = bf16[128,2,4,256]{0,3,2,1:T(8,128)(2,1)S(1)} fusion(f32[256,2,256]{0,2,1:T(8,128)} %get-tuple-element.154, bf16[1024,2,256]{0,2,1:T(8,128)(2,1)S(1)} %copy-done.1, bf16[256,1024,1]{0,1,2:T(8,128)(2,1)S(1)} %bitcast.90, bf16[128,4,2,256]{3,2,1,0:T(2,128)(2,1)S(1)} %bitcast.84, f32[256,2,192]{0,2,1:T(8,128)S(1)} %slice.59, ...), kind=kOutput, calls=%fused_computation.13 | convolution fusion | flops 403439616 | bytes 3997696 | tf_op jit(solution)/shard_map/jbil,cil->jibc/dot_general | solution.py:67
  104.8 0.0 copy-start.6
  104.8 1.2 copy.65
  106.0 19.0 %all-to-all-start.2 = ((bf16[128,2,4,256]{3,2,1,0:T(4,128)(2,1)}), bf16[128,2,4,256]{3,2,1,0:T(4,128)(2,1)S(1)}, u32[]{:S(2)}, u32[]{:S(2)}) async-start(bf16[128,2,4,256]{3,2,1,0:T(4,128)(2,1)} %copy.65), calls=%async_computation.2 | async-start | bytes 1048576 | tf_op jit(solution)/shard_map/all_to_all | solution.py:70
  125.0 1.2 dynamic-slice
  126.8 0.2 dynamic-update-slice
  127.1 37.2 %all-reduce.4 = s32[256]{0:T(256)S(1)} all-reduce(s32[256]{0:T(256)S(1)} %dynamic-update-slice), channel_id=1, replica_groups=mesh['section'=4,'trial'=128] {'trial'}, use_global_device_ids=true, to_apply=%add.4 | all-reduce | flops 256 | bytes 2048
  164.3 0.1 convert_reduce_fusion
  164.4 0.0 all-to-all-done.2
  164.4 0.1 copy.75
  164.5 13.8 %while.14 = (s32[]{:T(128)}, f32[128,1024]{1,0:T(8,128)S(1)}, s32[128]{0:T(128)S(1)}, s32[256]{0:T(256)S(1)}, f32[256,1024]{1,0:T(8,128)S(1)}, /*index=5*/s32[]{:T(128)}, s32[]{:T(128)}) while((s32[]{:T(128)}, f32[128,1024]{1,0:T(8,128)S(1)}, s32[128]{0:T(128)S(1)}, s32[256]{0:T(256)S(1)}, f32[256,1024]{1,0:T(8,128)S(1)}, ...), condition=%wide.region_2.3_spmd.clone, body=%wide.region_1.2_spmd.clone.sunk | while | flops 527491 | bytes 2630751 | solution.py:87
  164.6 1.3 gather_fusion.1
  165.9 0.8 gather_fusion
  166.7 0.2 select_add_fusion.2
  166.9 1.3 gather_fusion.1
  168.1 0.8 gather_fusion
  169.0 0.2 select_add_fusion.2
  169.2 1.3 gather_fusion.1
  170.4 0.8 gather_fusion
  171.3 0.2 select_add_fusion.2
  171.5 1.3 gather_fusion.1
  172.7 0.8 gather_fusion
  173.6 0.2 select_add_fusion.2
  173.7 1.3 gather_fusion.1
  175.0 0.8 gather_fusion
  175.8 0.2 select_add_fusion.2
  176.0 1.3 gather_fusion.1
  177.3 0.8 gather_fusion
  178.1 0.2 select_add_fusion.2
  178.3 0.9 convert_element_type.61
  (34 shorter events, 0.3 us)
Async XLA Ops:
  6.5 96.3 %copy-start = (bf16[512,2,256]{2,1,0:T(2,128)(2,1)S(1)}, bf16[512,2,256]{2,1,0:T(2,128)(2,1)}, u32[]{:S(2)}) copy-start(bf16[512,2,256]{2,1,0:T(2,128)(2,1)} %param.9) | copy-start | bytes 1572868
  6.5 3.4 %copy-start.3 = (bf16[3,1024,256]{2,1,0:T(8,128)(2,1)S(1)}, bf16[3,1024,256]{2,1,0:T(8,128)(2,1)}, u32[]{:S(2)}) copy-start(bf16[3,1024,256]{2,1,0:T(8,128)(2,1)} %param.14) | copy-start | bytes 4718596
  6.5 49.0 %all-gather.3.cloned.1.call-start = ((), (), s32[]{:S(2)}) async-start(), calls=%async_computation.3 | async-start | bytes 1310720 | tf_op jit(solution)/shard_map/all_gather | solution.py:41
  12.6 4.4 %copy-start.5 = (bf16[256,2,256]{2,1,0:T(2,128)(2,1)S(1)}, bf16[256,2,256]{2,1,0:T(2,128)(2,1)}, u32[]{:S(2)}) copy-start(bf16[256,2,256]{2,1,0:T(2,128)(2,1)} %param.10) | copy-start | bytes 786436
  12.6 33.6 %all-to-all-start = ((bf16[3,1024,256]{2,0,1:T(4,128)(2,1)}), bf16[3,1024,256]{2,0,1:T(4,128)(2,1)S(1)}, u32[]{:S(2)}, u32[]{:S(2)}) async-start(bf16[3,1024,256]{2,0,1:T(4,128)(2,1)} %copy.52), calls=%async_computation | async-start | bytes 4194304 | tf_op jit(solution)/shard_map/all_to_all | solution.py:56
  17.0 83.5 %all-gather.5.cloned.1.call-start = ((), (), s32[]{:S(2)}) async-start(), calls=%async_computation.4 | async-start | bytes 1310720 | tf_op jit(solution)/shard_map/all_gather | solution.py:41
  55.6 1.8 copy-start.2
  57.9 1.5 copy-start.4
  100.5 1.8 copy-start.1
  104.8 22.1 %copy-start.6 = (s32[2]{0:T(128)S(1)}, s32[2]{0:T(128)}, u32[]{:S(2)}) copy-start(s32[2]{0:T(128)} %param.15) | copy-start | bytes 28
  106.0 58.4 %all-to-all-start.2 = ((bf16[128,2,4,256]{3,2,1,0:T(4,128)(2,1)}), bf16[128,2,4,256]{3,2,1,0:T(4,128)(2,1)S(1)}, u32[]{:S(2)}, u32[]{:S(2)}) async-start(bf16[128,2,4,256]{3,2,1,0:T(4,128)(2,1)} %copy.65), calls=%async_computation.2 | async-start | bytes 1048576 | tf_op jit(solution)/shard_map/all_to_all | solution.py:70
Sparse Core Ops, SparseCore 0:
  10.0 45.5 all-gather.2
  59.5 40.9 all-gather.4
where the time goes:
time: 187 us; the launch traced here: 186 us
  blocking collectives  68.8 us (37%)
  waiting for transfers between devices  42.5 us (23%)
  local copies, waits for them, and re-layouts  26.8 us (14%)
  starting transfers between devices  23.4 us (13%)
  between operations  14.2 us (8%)
  matrix products  7.88 us (4%)
  other arithmetic  2.14 us (1%)
    unnamed x1, blocking collectives  37.2 us
    all_to_all x1, blocking collectives, body(): lax.all_to_all(first_kernel, 'section', split_axis=1, concat_axis=2, tile...  31.6 us
    all_to_all x1, waiting for transfers between devices, body(): lax.all_to_all(second_kernel, 'section', split_axis=1, concat_axis=2, til...  29 us
    all_to_all x1, starting transfers between devices, body(): lax.all_to_all(partials.astype(jnp.bfloat16), 'trial', split_axis=0, conc...  19 us
    all_gather x2, waiting for transfers between devices, layer_backprop(): lax.all_gather(flow_grad, 'section', axis=0, tiled=True)  13.4 us
    unnamed x23, local copies, waits for them, and re-layouts  8.19 us
    gather x6, local copies, waits for them, and re-layouts, add_offset(): jnp.take(every_id, clipped, axis=0) == session_list  7.59 us
    dot_general x5, matrix products, tap_sum(): lax.dot_general(weights[kernel_tap], flow_grad, (((1,), (0,)), ((), ())),...  5.91 us
  transfers between devices with their start and end apart: 4, of which 3 were waited for; matrix products, arithmetic and copies ran while one was open for 5% of the time, Pallas kernels for 0%

commit v1 on v0

--- a/solution.py
+++ b/solution.py
@@ -7,6 +7,27 @@
 FIRST_DILATION = 32
 SECOND_DILATION = 64
 MOST = 6
+
+
+def collect(value, axis, dim):
+    devices, mine, rows = (lax.axis_size(axis), lax.axis_index(axis), value.shape[dim])
+    right = [(i, (i + 1) % devices) for i in range(devices)]
+    behind = [(i, (i - 1) % devices) for i in range(devices)]
+    out = jnp.zeros((*value.shape[:dim], devices * rows, *value.shape[dim + 1 :]), value.dtype)
+    out = lax.dynamic_update_slice_in_dim(out, value, mine * rows, axis=dim)
+    from_left = from_right = value
+    half = devices // 2
+    for step in range(1, half + 1):
+        from_left = lax.ppermute(from_left, axis, right)
+        out = lax.dynamic_update_slice_in_dim(
+            out, from_left, (mine - step) % devices * rows, axis=dim
+        )
+        if step < devices - half:
+            from_right = lax.ppermute(from_right, axis, behind)
+            out = lax.dynamic_update_slice_in_dim(
+                out, from_right, (mine + step) % devices * rows, axis=dim
+            )
+    return out
 
 
 def gelu_slope(preact):
@@ -38,7 +59,7 @@
 
 def layer_backprop(upstream, preact, turned, spacing):
     flow_grad = (upstream.astype(jnp.float32) * gelu_slope(preact)).astype(jnp.bfloat16)
-    back_sum = tap_sum(turned, lax.all_gather(flow_grad, "section", axis=0, tiled=True), spacing)
+    back_sum = tap_sum(turned, collect(flow_grad, "section", 0), spacing)
     return (upstream.astype(jnp.float32) + back_sum).astype(jnp.bfloat16)
 
 

time: 187 us -> 178 us (0.952)
  blocking collectives: 68.8 us -> 37 us
  starting transfers between devices: 23.4 us -> 46.6 us
  local copies, waits for them, and re-layouts: 26.8 us -> 43.2 us
  between operations: 14.2 us -> 1.09 us
  waiting for transfers between devices: 42.5 us -> 38.5 us
    all_to_all x1 -> x0, blocking collectives: 31.6 us -> none  [body(): lax.all_to_all(first_kernel, 'section', split_axis=1, concat_axis=2, tile...]
    ppermute x0 -> x6, waiting for transfers between devices: none -> 30.5 us  [the longest x4 30.5 us: collect(): from_left = lax.ppermute(from_left, axis, right)]
    all_to_all x1, waiting for transfers between devices: 29 us -> 0.01 us  [body(): lax.all_to_all(second_kernel, 'section', split_axis=1, concat_axis=2, til...]
    ppermute x0 -> x6, starting transfers between devices: none -> 18.1 us  [the longest x4 11.7 us: collect(): from_left = lax.ppermute(from_left, axis, right)]
    all_gather x2 -> x0, waiting for transfers between devices: 13.4 us -> none  [layer_backprop(): lax.all_gather(flow_grad, 'section', axis=0, tiled=True)]
    all_to_all x0 -> x1, waiting for transfers between devices: none -> 8.03 us  [body(): lax.all_to_all(first_kernel, 'section', split_axis=1, concat_axis=2, tile...]
    dynamic_update_slice x0 -> x6, local copies, waits for them, and re-layouts: none -> 4.89 us  [the longest x4 2.94 us: collect(): lax.dynamic_update_slice_in_dim(out, from_left, (mine - step) % devices *...]
    all_to_all x0 -> x1, starting transfers between devices: none -> 4.46 us  [body(): lax.all_to_all(first_kernel, 'section', split_axis=1, concat_axis=2, tile...]
  transfers between devices with their start and end apart: 4 -> 9, of which waited for: 3 -> 5; matrix products, arithmetic and copies ran while one was open for 5% -> 17% of each run, Pallas kernels for 0% -> 0%
where the time goes in v1:
time: 178 us; the launch traced here: 177 us
  starting transfers between devices  46.6 us (26%)
  local copies, waits for them, and re-layouts  43.2 us (24%)
  waiting for transfers between devices  38.5 us (22%)
  blocking collectives  37 us (21%)
  matrix products  7.5 us (4%)
  other arithmetic  3.11 us (2%)
    unnamed x1, blocking collectives  37 us
    ppermute x4, waiting for transfers between devices, collect(): from_left = lax.ppermute(from_left, axis, right)  30.5 us
    all_to_all x1, starting transfers between devices, body(): lax.all_to_all(partials.astype(jnp.bfloat16), 'trial', split_axis=0, conc...  19.5 us
    unnamed x21, local copies, waits for them, and re-layouts  12.2 us
    ppermute x4, starting transfers between devices, collect(): from_left = lax.ppermute(from_left, axis, right)  11.7 us
    all_to_all x1, waiting for transfers between devices, body(): lax.all_to_all(first_kernel, 'section', split_axis=1, concat_axis=2, tile...  8.03 us
    gather x6, local copies, waits for them, and re-layouts, add_offset(): jnp.take(every_id, clipped, axis=0) == session_list  7.59 us
    ppermute x2, starting transfers between devices, collect(): from_right = lax.ppermute(from_right, axis, behind)  6.36 us
  transfers between devices with their start and end apart: 9, of which 5 were waited for; matrix products, arithmetic and copies ran while one was open for 17% of the time, Pallas kernels for 0%

profile of v1, /device:TPU:8, one launch (start us, length us, event | category | flops | bytes accessed | tf_op | source)
XLA Modules:
  0.0 177.5 jit_solution(13010133923192974474)
XLA Ops:
  0.0 4.1 %copy.52 = bf16[3,1024,256]{2,0,1:T(4,128)(2,1)} copy(bf16[3,1024,256]{2,1,0:T(8,128)(2,1)} %param.14) | data formatting | bytes 3145728 | tf_op args[5]
  4.1 4.6 %all-to-all-start = ((bf16[3,1024,256]{2,0,1:T(4,128)(2,1)}), bf16[3,1024,256]{2,0,1:T(4,128)(2,1)}, u32[]{:S(2)}, u32[]{:S(2)}) async-start(bf16[3,1024,256]{2,0,1:T(4,128)(2,1)} %copy.52), calls=%async_computation | async-start | bytes 4194304 | tf_op jit(solution)/shard_map/all_to_all | solution.py:77
  8.7 0.2 copy.50
  8.9 0.9 copy.51
  10.0 1.9 %constant_dynamic-update-slice_fusion.7 = (bf16[1024,2,256]{0,2,1:T(8,128)(2,1)S(1)}, bf16[256,2,256]{0,2,1:T(8,128)(2,1)}) fusion(bf16[1024,2,256]{0,2,1:T(8,128)(2,1)S(1)} %broadcast.155.clone, s32[]{:T(128)S(6)} %select_n.94, bf16[256,2,256]{0,2,1:T(8,128)(2,1)} %copy.51, bf16[256,2,256]{0,2,1:T(8,128)(2,1)S(1)} %copy.50), kind=kLoop, calls=%fused_computation.66 | loop fusion | flops 1572864 | bytes 1048580 | tf_op jit(solution)/shard_map/dynamic_update_slice | solution.py:17
  11.9 3.9 %collective-permute-start = (bf16[256,2,256]{0,2,1:T(8,128)(2,1)}, bf16[256,2,256]{0,2,1:T(8,128)(2,1)}, u32[]{:S(2)}, u32[]{:S(2)}) collective-permute-start(bf16[256,2,256]{0,2,1:T(8,128)(2,1)} %get-tuple-element.150), channel_id=1, source_target_pairs={{0,128},{128,256},{256,384},{384,0},{1,129},{129,257},{257,385},{3... | collective-permute-start | bytes 786440 | tf_op jit(solution)/shard_map/ppermute | solution.py:21
  15.7 3.2 %collective-permute-start.1 = (bf16[256,2,256]{0,2,1:T(8,128)(2,1)}, bf16[256,2,256]{0,2,1:T(8,128)(2,1)}, u32[]{:S(2)}, u32[]{:S(2)}) collective-permute-start(bf16[256,2,256]{0,2,1:T(8,128)(2,1)} %get-tuple-element.150), channel_id=1, source_target_pairs={{0,384},{128,0},{256,128},{384,256},{1,385},{129,1},{257,129},{385... | collective-permute-start | bytes 786440 | tf_op jit(solution)/shard_map/ppermute | solution.py:26
  18.9 21.8 %collective-permute-done = bf16[256,2,256]{0,2,1:T(8,128)(2,1)} collective-permute-done((bf16[256,2,256]{0,2,1:T(8,128)(2,1)}, bf16[256,2,256]{0,2,1:T(8,128)(2,1)}, u32[]{:S(2)}, u32[]{:S(2)}) %collective-permute-start) | collective-permute-done | bytes 262176 | tf_op jit(solution)/shard_map/ppermute | solution.py:21
  40.7 1.9 %collective-permute-start.2 = (bf16[256,2,256]{0,2,1:T(8,128)(2,1)}, bf16[256,2,256]{0,2,1:T(8,128)(2,1)}, u32[]{:S(2)}, u32[]{:S(2)}) collective-permute-start(bf16[256,2,256]{0,2,1:T(8,128)(2,1)} %collective-permute-done), channel_id=1, source_target_pairs={{0,128},{128,256},{256,384},{384,0},{1,129},{129,257},{257,385},{3... | collective-permute-start | bytes 786440 | tf_op jit(solution)/shard_map/ppermute | solution.py:21
  42.7 1.8 %copy.54 = bf16[256,2,256]{0,2,1:T(8,128)(2,1)} copy(bf16[256,2,256]{2,1,0:T(2,128)(2,1)} %param.10) | data formatting | bytes 524288 | tf_op args[1]
  44.5 2.7 %copy.55 = bf16[3,1024,256]{2,0,1:T(4,128)(2,1)} copy(bf16[3,1024,256]{2,1,0:T(8,128)(2,1)S(1)} %copy-done.2) | data formatting | bytes 3145728 | tf_op args[4]
  47.2 1.0 constant_dynamic-update-slice_fusion.6
  48.2 1.0 constant_dynamic-update-slice_fusion.5
  49.2 2.1 %collective-permute-done.2 = bf16[256,2,256]{0,2,1:T(8,128)(2,1)} collective-permute-done((bf16[256,2,256]{0,2,1:T(8,128)(2,1)}, bf16[256,2,256]{0,2,1:T(8,128)(2,1)}, u32[]{:S(2)}, u32[]{:S(2)}) %collective-permute-start.2) | collective-permute-done | bytes 262176 | tf_op jit(solution)/shard_map/ppermute | solution.py:21
  51.3 1.0 constant_dynamic-update-slice_fusion.4
  52.3 4.5 %all-to-all-start.1 = ((bf16[3,1024,256]{2,0,1:T(4,128)(2,1)}), bf16[3,1024,256]{2,0,1:T(4,128)(2,1)}, u32[]{:S(2)}, u32[]{:S(2)}) async-start(bf16[3,1024,256]{2,0,1:T(4,128)(2,1)} %copy.55), calls=%async_computation.1 | async-start | bytes 4194304 | tf_op jit(solution)/shard_map/all_to_all | solution.py:76
  56.8 3.1 %copy.79 = bf16[3,4,256,256]{3,1,2,0:T(4,128)(2,1)S(1)} copy(bf16[3,4,256,256]{3,0,2,1:T(4,128)(2,1)} %bitcast.1) | data formatting | bytes 3145728 | tf_op jit(solution)/shard_map/all_to_all | solution.py:77
  59.8 0.5 fusion.36
  60.4 1.2 reshape.105
  61.6 1.5 convolution_bitcast_fusion.4
  63.1 0.8 copy-done.1
  63.9 0.4 reshape.106
  64.2 0.5 convolution_bitcast_fusion.3
  64.7 0.7 slice.54
  65.5 1.2 reshape.104
  66.8 2.6 %constant_dynamic-update-slice_fusion.3 = (bf16[1024,2,256]{0,2,1:T(8,128)(2,1)S(1)}, bf16[256,2,256]{0,2,1:T(8,128)(2,1)}, f32[256,2,256]{0,2,1:T(8,128)}) fusion(bf16[1024,2,256]{0,2,1:T(8,128)(2,1)S(1)} %broadcast.155, s32[]{:T(128)S(6)} %select_n.94, bf16[256,2,256]{0,2,1:T(8,128)(2,1)} %copy.54, f32[256,2,128]{0,2,1:T(8,128)} %slice.54, ...), kind=kOutput, calls=%fused_computation.62 | convolution fusion | flops 270663680 | bytes 3801092 | tf_op jit(solution)/shard_map/dot_general | solution.py:48
  69.4 3.9 %collective-permute-start.3 = (bf16[256,2,256]{0,2,1:T(8,128)(2,1)}, bf16[256,2,256]{0,2,1:T(8,128)(2,1)S(1)}, u32[]{:S(2)}, u32[]{:S(2)}) collective-permute-start(bf16[256,2,256]{0,2,1:T(8,128)(2,1)} %get-tuple-element.148), channel_id=1, source_target_pairs={{0,128},{128,256},{256,384},{384,0},{1,129},{129,257},{257,385},{3... | collective-permute-start | bytes 786440 | tf_op jit(solution)/shard_map/ppermute | solution.py:21
  73.3 3.2 %collective-permute-start.4 = (bf16[256,2,256]{0,2,1:T(8,128)(2,1)}, bf16[256,2,256]{0,2,1:T(8,128)(2,1)}, u32[]{:S(2)}, u32[]{:S(2)}) collective-permute-start(bf16[256,2,256]{0,2,1:T(8,128)(2,1)} %get-tuple-element.148), channel_id=1, source_target_pairs={{0,384},{128,0},{256,128},{384,256},{1,385},{129,1},{257,129},{385... | collective-permute-start | bytes 786440 | tf_op jit(solution)/shard_map/ppermute | solution.py:26
  76.5 8.0 %all-to-all-done.1 = bf16[3,1024,256]{2,0,1:T(4,128)(2,1)} async-done(((bf16[3,1024,256]{2,0,1:T(4,128)(2,1)}), bf16[3,1024,256]{2,0,1:T(4,128)(2,1)}, u32[]{:S(2)}, u32[]{:S(2)}) %all-to-all-start.1) | async-done | bytes 1572896 | tf_op jit(solution)/shard_map/all_to_all | solution.py:76
  84.5 1.8 %copy.56 = bf16[3,1024,256]{2,1,0:T(8,128)(2,1)S(1)} copy(bf16[3,1024,256]{2,0,1:T(4,128)(2,1)} %all-to-all-done.1) | data formatting | bytes 3145728 | tf_op jit(solution)/shard_map/all_to_all | solution.py:76
  86.3 0.8 collective-permute-done.3
  87.1 2.1 %collective-permute-start.5 = (bf16[256,2,256]{0,2,1:T(8,128)(2,1)S(1)}, bf16[256,2,256]{0,2,1:T(8,128)(2,1)}, u32[]{:S(2)}, u32[]{:S(2)}) collective-permute-start(bf16[256,2,256]{0,2,1:T(8,128)(2,1)S(1)} %collective-permute-done.3), channel_id=1, source_target_pairs={{0,128},{128,256},{256,384},{384,0},{1,129},{129,257},{257,385},{3... | collective-permute-start | bytes 786440 | tf_op jit(solution)/shard_map/ppermute | solution.py:21
  89.2 0.9 fusion.35
  90.1 0.2 copy.59
  90.4 0.2 copy.61
  90.6 1.2 copy.57
  91.9 1.0 constant_dynamic-update-slice_fusion.1
  92.8 5.7 %collective-permute-done.5 = bf16[256,2,256]{0,2,1:T(8,128)(2,1)} collective-permute-done((bf16[256,2,256]{0,2,1:T(8,128)(2,1)S(1)}, bf16[256,2,256]{0,2,1:T(8,128)(2,1)}, u32[]{:S(2)}, u32[]{:S(2)}) %collective-permute-start.5) | collective-permute-done | bytes 262176 | tf_op jit(solution)/shard_map/ppermute | solution.py:21
  98.6 1.0 constant_dynamic-update-slice_fusion
  99.6 0.4 convolution_bitcast_fusion.1
  100.0 0.4 convolution_bitcast_fusion
  100.5 2.0 %fusion.3 = bf16[128,2,4,256]{0,3,2,1:T(8,128)(2,1)S(1)} fusion(f32[256,2,256]{0,2,1:T(8,128)} %get-tuple-element.157, bf16[1024,2,256]{0,2,1:T(8,128)(2,1)S(1)} %constant_dynamic-update-slice_fusion, bf16[256,1024,1]{0,1,2:T(8,128)(2,1)S(1)} %bitcast.89, bf16[128,4,2,256]{3,2,1,0:T(2,128)(2,1)S(1)} %bitcast.84, f32[256,2,192]{0,2,1:T(8,128)S(1)} %slice.59, ...), kind=kOutput, calls=%fused_computation.13 | convolution fusion | flops 403439616 | bytes 3997696 | tf_op jit(solution)/shard_map/jbil,cil->jibc/dot_general | solution.py:88
  102.5 1.2 copy.65
  103.7 19.5 %all-to-all-start.2 = ((bf16[128,2,4,256]{3,2,1,0:T(4,128)(2,1)}), bf16[128,2,4,256]{3,2,1,0:T(4,128)(2,1)S(1)}, u32[]{:S(2)}, u32[]{:S(2)}) async-start(bf16[128,2,4,256]{3,2,1,0:T(4,128)(2,1)} %copy.65), calls=%async_computation.2 | async-start | bytes 1048576 | tf_op jit(solution)/shard_map/all_to_all | solution.py:91
  123.3 1.3 dynamic-slice
  125.2 0.2 dynamic-update-slice
  125.5 37.0 %all-reduce.4 = s32[256]{0:T(256)S(1)} all-reduce(s32[256]{0:T(256)S(1)} %dynamic-update-slice), channel_id=1, replica_groups=mesh['section'=4,'trial'=128] {'trial'}, use_global_device_ids=true, to_apply=%add.4 | all-reduce | flops 256 | bytes 2048
  162.8 13.8 %while.14 = (s32[]{:T(128)}, f32[128,1024]{1,0:T(8,128)S(1)}, s32[128]{0:T(128)S(1)}, s32[256]{0:T(256)S(1)}, f32[256,1024]{1,0:T(8,128)S(1)}, /*index=5*/s32[]{:T(128)}, s32[]{:T(128)}) while((s32[]{:T(128)}, f32[128,1024]{1,0:T(8,128)S(1)}, s32[128]{0:T(128)S(1)}, s32[256]{0:T(256)S(1)}, f32[256,1024]{1,0:T(8,128)S(1)}, ...), condition=%wide.region_2.3_spmd.clone, body=%wide.region_1.2_spmd.clone.sunk | while | flops 527491 | bytes 2630751 | solution.py:108
  162.8 1.3 gather_fusion.1
  164.1 0.8 gather_fusion
  164.9 0.2 select_add_fusion.2
  165.1 1.3 gather_fusion.1
  166.4 0.8 gather_fusion
  167.2 0.2 select_add_fusion.2
  167.4 1.3 gather_fusion.1
  168.7 0.8 gather_fusion
  169.5 0.2 select_add_fusion.2
  169.7 1.3 gather_fusion.1
  171.0 0.8 gather_fusion
  172.0 1.3 gather_fusion.1
  173.3 0.8 gather_fusion
  174.3 1.3 gather_fusion.1
  175.6 0.8 gather_fusion
  176.6 0.9 convert_element_type.61
  (48 shorter events, 1.2 us)
Async XLA Ops:
  0.0 100.5 %copy-start = (bf16[512,2,256]{2,1,0:T(2,128)(2,1)S(1)}, bf16[512,2,256]{2,1,0:T(2,128)(2,1)}, u32[]{:S(2)}) copy-start(bf16[512,2,256]{2,1,0:T(2,128)(2,1)} %param.9) | copy-start | bytes 1572868
  4.1 4.6 %copy-start.3 = (bf16[256,2,256]{2,1,0:T(2,128)(2,1)S(1)}, bf16[256,2,256]{2,1,0:T(2,128)(2,1)}, u32[]{:S(2)}) copy-start(bf16[256,2,256]{2,1,0:T(2,128)(2,1)} %param.12) | copy-start | bytes 786436
  4.1 4.8 %copy-start.4 = (bf16[256,2,256]{2,1,0:T(2,128)(2,1)S(1)}, bf16[256,2,256]{2,1,0:T(2,128)(2,1)}, u32[]{:S(2)}) copy-start(bf16[256,2,256]{2,1,0:T(2,128)(2,1)} %param.11) | copy-start | bytes 786436
  4.1 48.2 %all-to-all-start = ((bf16[3,1024,256]{2,0,1:T(4,128)(2,1)}), bf16[3,1024,256]{2,0,1:T(4,128)(2,1)}, u32[]{:S(2)}, u32[]{:S(2)}) async-start(bf16[3,1024,256]{2,0,1:T(4,128)(2,1)} %copy.52), calls=%async_computation | async-start | bytes 4194304 | tf_op jit(solution)/shard_map/all_to_all | solution.py:77
  8.9 35.6 %copy-start.2 = (bf16[3,1024,256]{2,1,0:T(8,128)(2,1)S(1)}, bf16[3,1024,256]{2,1,0:T(8,128)(2,1)}, u32[]{:S(2)}) copy-start(bf16[3,1024,256]{2,1,0:T(8,128)(2,1)} %param.13) | copy-start | bytes 4718596
  11.9 28.9 %collective-permute-start = (bf16[256,2,256]{0,2,1:T(8,128)(2,1)}, bf16[256,2,256]{0,2,1:T(8,128)(2,1)}, u32[]{:S(2)}, u32[]{:S(2)}) collective-permute-start(bf16[256,2,256]{0,2,1:T(8,128)(2,1)} %get-tuple-element.150), channel_id=1, source_target_pairs={{0,128},{128,256},{256,384},{384,0},{1,129},{129,257},{257,385},{3... | collective-permute-start | bytes 786440 | tf_op jit(solution)/shard_map/ppermute | solution.py:21
  15.7 32.4 %collective-permute-start.1 = (bf16[256,2,256]{0,2,1:T(8,128)(2,1)}, bf16[256,2,256]{0,2,1:T(8,128)(2,1)}, u32[]{:S(2)}, u32[]{:S(2)}) collective-permute-start(bf16[256,2,256]{0,2,1:T(8,128)(2,1)} %get-tuple-element.150), channel_id=1, source_target_pairs={{0,384},{128,0},{256,128},{384,256},{1,385},{129,1},{257,129},{385... | collective-permute-start | bytes 786440 | tf_op jit(solution)/shard_map/ppermute | solution.py:26
  40.7 10.6 %collective-permute-start.2 = (bf16[256,2,256]{0,2,1:T(8,128)(2,1)}, bf16[256,2,256]{0,2,1:T(8,128)(2,1)}, u32[]{:S(2)}, u32[]{:S(2)}) collective-permute-start(bf16[256,2,256]{0,2,1:T(8,128)(2,1)} %collective-permute-done), channel_id=1, source_target_pairs={{0,128},{128,256},{256,384},{384,0},{1,129},{129,257},{257,385},{3... | collective-permute-start | bytes 786440 | tf_op jit(solution)/shard_map/ppermute | solution.py:21
  52.3 32.2 %all-to-all-start.1 = ((bf16[3,1024,256]{2,0,1:T(4,128)(2,1)}), bf16[3,1024,256]{2,0,1:T(4,128)(2,1)}, u32[]{:S(2)}, u32[]{:S(2)}) async-start(bf16[3,1024,256]{2,0,1:T(4,128)(2,1)} %copy.55), calls=%async_computation.1 | async-start | bytes 4194304 | tf_op jit(solution)/shard_map/all_to_all | solution.py:76
  63.1 0.8 copy-start.1
  64.7 2.0 %slice-start = ((f32[256,2,256]{0,2,1:T(8,128)}), f32[256,2,192]{0,2,1:T(8,128)S(1)}, s32[]{:S(2)}) async-start(f32[256,2,256]{0,2,1:T(8,128)} %copy-done.1), calls=%async_computation.3 | async-start | bytes 786432 | tf_op jit(solution)/shard_map/slice | solution.py:42
  69.4 17.7 %collective-permute-start.3 = (bf16[256,2,256]{0,2,1:T(8,128)(2,1)}, bf16[256,2,256]{0,2,1:T(8,128)(2,1)S(1)}, u32[]{:S(2)}, u32[]{:S(2)}) collective-permute-start(bf16[256,2,256]{0,2,1:T(8,128)(2,1)} %get-tuple-element.148), channel_id=1, source_target_pairs={{0,128},{128,256},{256,384},{384,0},{1,129},{129,257},{257,385},{3... | collective-permute-start | bytes 786440 | tf_op jit(solution)/shard_map/ppermute | solution.py:21
  73.3 18.6 %collective-permute-start.4 = (bf16[256,2,256]{0,2,1:T(8,128)(2,1)}, bf16[256,2,256]{0,2,1:T(8,128)(2,1)}, u32[]{:S(2)}, u32[]{:S(2)}) collective-permute-start(bf16[256,2,256]{0,2,1:T(8,128)(2,1)} %get-tuple-element.148), channel_id=1, source_target_pairs={{0,384},{128,0},{256,128},{384,256},{1,385},{129,1},{257,129},{385... | collective-permute-start | bytes 786440 | tf_op jit(solution)/shard_map/ppermute | solution.py:26
  87.1 11.4 %collective-permute-start.5 = (bf16[256,2,256]{0,2,1:T(8,128)(2,1)S(1)}, bf16[256,2,256]{0,2,1:T(8,128)(2,1)}, u32[]{:S(2)}, u32[]{:S(2)}) collective-permute-start(bf16[256,2,256]{0,2,1:T(8,128)(2,1)S(1)} %collective-permute-done.3), channel_id=1, source_target_pairs={{0,128},{128,256},{256,384},{384,0},{1,129},{129,257},{257,385},{3... | collective-permute-start | bytes 786440 | tf_op jit(solution)/shard_map/ppermute | solution.py:21
  102.5 22.7 %copy-start.5 = (s32[2]{0:T(128)S(1)}, s32[2]{0:T(128)}, u32[]{:S(2)}) copy-start(s32[2]{0:T(128)} %param.15) | copy-start | bytes 28
  103.7 58.9 %all-to-all-start.2 = ((bf16[128,2,4,256]{3,2,1,0:T(4,128)(2,1)}), bf16[128,2,4,256]{3,2,1,0:T(4,128)(2,1)S(1)}, u32[]{:S(2)}, u32[]{:S(2)}) async-start(bf16[128,2,4,256]{3,2,1,0:T(4,128)(2,1)} %copy.65), calls=%async_computation.2 | async-start | bytes 1048576 | tf_op jit(solution)/shard_map/all_to_all | solution.py:91
